TPU v7x, 128 devices: a whole 4x4x4 slice. The times are simulated.
128 devices in a mesh: ha: 16 (over z, y_lo, core), wa: 8 (over x, y_hi).
Axes of the slice: x: 4, y: 4 (y_hi: 2, y_lo: 2; y = y_hi * 2 + y_lo), z: 4, core: 2. Of those that a mesh axis runs over, the one named last changes fastest.
Arguments:
- tokens: bfloat16 [256, 256, 512], P('ha', 'wa'), may hold values from -40 to 40
- cotangent: bfloat16 [256, 256, 512], P('ha', 'wa'), may hold values from -6 to 6
- norm_gain: float32 [512], replicated, may hold values from 0.1 to 1.9
- in_weight: bfloat16 [512, 1536], replicated, may hold values from -0.25 to 0.25
- out_weight: bfloat16 [512, 512], replicated, may hold values from -0.25 to 0.25
- bias_table: float32 [16, 31, 31], replicated, may hold values from -256 to 256
Outputs:
- grad_input: bfloat16 [256, 256, 512], P('ha', 'wa')
- grad_table: float32 [16, 31, 31], replicated
All inputs are finite; a program needn't handle non-finite values.
Results may differ from a plain program's by a relative error of at most 0.011.
Values may be sent and summed in bfloat16 or wider, within the bound.
No kernel may reach another device: no remote copies, remote signals or barrier semaphores. Data moves between devices by JAX's collectives and lax.ppermute only.
A program may use at most 128 MiB of HBM per device.

v0:
```python
import jax
import jax.numpy as jnp
from jax import lax
from jax.sharding import PartitionSpec as P

D = 512
HEADS = 16
HEAD_DIM = 32
WIN = 16
TAB = 31
NORM_EPS = 1e-05


def offset_hot():
    places = jnp.arange(WIN)
    slot_ids = jnp.arange(TAB)
    return (
        places[:, None, None] - places[None, :, None] + (WIN - 1) == slot_ids[None, None, :]
    ).astype(jnp.float32)


def full_bias(bias_table, offset_table):
    partial_rows = jnp.einsum(
        "abd,hde->habe", offset_table, bias_table, precision=lax.Precision.HIGHEST
    )
    spread = jnp.einsum(
        "uve,habe->haubv", offset_table, partial_rows, precision=lax.Precision.HIGHEST
    )
    return spread.reshape(HEADS, WIN * WIN, WIN * WIN)


def group_grad(group_tokens, group_cot, norm_gain, in_weight, out_weight, bias_full, offset_table):
    group_rows = WIN * WIN
    tokens_wide = group_tokens.astype(jnp.float32)
    center = jnp.mean(tokens_wide, axis=-1, keepdims=True)
    shifted = tokens_wide - center
    inv_std = lax.rsqrt(jnp.mean(shifted * shifted, axis=-1, keepdims=True) + NORM_EPS)
    unit_rows = shifted * inv_std
    normed = (unit_rows * norm_gain).astype(jnp.bfloat16)
    mixed_rows = jnp.dot(normed, in_weight, preferred_element_type=jnp.float32)
    query_scale = HEAD_DIM ** (-0.5)
    queries = (
        (mixed_rows[:, :D] * query_scale).astype(jnp.bfloat16).reshape(group_rows, HEADS, HEAD_DIM)
    )
    key_rows = mixed_rows[:, D : 2 * D].astype(jnp.bfloat16).reshape(group_rows, HEADS, HEAD_DIM)
    values = mixed_rows[:, 2 * D :].astype(jnp.bfloat16).reshape(group_rows, HEADS, HEAD_DIM)
    scores = (
        jnp.einsum("thd,shd->hts", queries, key_rows, preferred_element_type=jnp.float32)
        + bias_full
    )
    row_top = jnp.max(scores, axis=-1, keepdims=True)
    exponent = jnp.exp(scores - row_top)
    attn_probs = exponent / jnp.sum(exponent, axis=-1, keepdims=True)
    probs_half = attn_probs.astype(jnp.bfloat16)
    grad_out = lax.dot_general(
        group_cot, out_weight, (((1,), (1,)), ((), ())), preferred_element_type=jnp.float32
    )
    grad_out = grad_out.astype(jnp.bfloat16).reshape(group_rows, HEADS, HEAD_DIM)
    grad_probs = jnp.einsum("thd,shd->hts", grad_out, values, preferred_element_type=jnp.float32)
    grad_values = jnp.einsum(
        "hts,thd->shd", probs_half, grad_out, preferred_element_type=jnp.float32
    ).astype(jnp.bfloat16)
    grad_scores = attn_probs * (
        grad_probs - jnp.sum(attn_probs * grad_probs, axis=-1, keepdims=True)
    )
    scores_half = grad_scores.astype(jnp.bfloat16)
    grad_queries = (
        jnp.einsum("hts,shd->thd", scores_half, key_rows, preferred_element_type=jnp.float32)
        * query_scale
    ).astype(jnp.bfloat16)
    grad_keys = jnp.einsum(
        "hts,thd->shd", scores_half, queries, preferred_element_type=jnp.float32
    ).astype(jnp.bfloat16)
    grad_mixed = jnp.concatenate(
        [
            grad_queries.reshape(group_rows, D),
            grad_keys.reshape(group_rows, D),
            grad_values.reshape(group_rows, D),
        ],
        axis=1,
    )
    grad_normed = lax.dot_general(
        grad_mixed, in_weight, (((1,), (1,)), ((), ())), preferred_element_type=jnp.float32
    )
    grad_unit = grad_normed * norm_gain
    grad_rows = inv_std * (
        grad_unit
        - jnp.mean(grad_unit, axis=-1, keepdims=True)
        - unit_rows * jnp.mean(grad_unit * unit_rows, axis=-1, keepdims=True)
    )
    folded = jnp.einsum(
        "haubv,uve->habe",
        grad_scores.reshape(HEADS, WIN, WIN, WIN, WIN),
        offset_table,
        precision=lax.Precision.HIGHEST,
    )
    table_part = jnp.einsum("habe,abd->hde", folded, offset_table, precision=lax.Precision.HIGHEST)
    return (grad_rows.astype(jnp.bfloat16), table_part)


def body(tokens, cotangent, norm_gain, in_weight, out_weight, bias_table):
    offset_table = offset_hot()
    bias_full = full_bias(bias_table, offset_table)
    high_parts = lax.axis_size("ha")
    wide_parts = lax.axis_size("wa")
    rows_local, cols_local, channels = tokens.shape
    row_steps = WIN // high_parts
    col_steps = WIN // wide_parts
    stride_h = rows_local // row_steps
    stride_w = cols_local // col_steps
    row_groups = stride_h // high_parts
    col_groups = stride_w // wide_parts
    group_count = row_groups * col_groups

    def to_layout(tile_block):
        laid = tile_block.reshape(
            row_steps, high_parts, row_groups, col_steps, wide_parts, col_groups, channels
        )
        laid = laid.transpose(2, 5, 1, 4, 0, 3, 6)
        return laid.reshape(group_count, high_parts, wide_parts, row_steps, col_steps, channels)

    def one_group(pair_rows):
        return group_grad(
            pair_rows[0], pair_rows[1], norm_gain, in_weight, out_weight, bias_full, offset_table
        )

    laid_tokens = to_layout(tokens)
    laid_cot = to_layout(cotangent)

    def swap_rows(laid):
        items = laid.shape[0]
        shaped = laid.reshape(items, high_parts, wide_parts, row_steps, col_steps, channels)
        return shaped.transpose(0, 1, 3, 2, 4, 5).reshape(items, WIN * WIN, channels)

    flat_shape = (group_count, high_parts * wide_parts, row_steps * col_steps, channels)
    grad_rows, table_parts = lax.map(
        one_group,
        (
            swap_rows(
                lax.all_to_all(
                    laid_tokens.reshape(flat_shape),
                    ("ha", "wa"),
                    split_axis=1,
                    concat_axis=1,
                    tiled=True,
                )
            ),
            swap_rows(
                lax.all_to_all(
                    laid_cot.reshape(flat_shape),
                    ("ha", "wa"),
                    split_axis=1,
                    concat_axis=1,
                    tiled=True,
                )
            ),
        ),
    )
    items = grad_rows.shape[0]
    shaped = grad_rows.reshape(items, high_parts, row_steps, wide_parts, col_steps, channels)
    grads_laid, table_parts = (
        shaped.transpose(0, 1, 3, 2, 4, 5).reshape(
            items, high_parts * wide_parts, row_steps * col_steps, channels
        ),
        table_parts,
    )
    returned = lax.all_to_all(grads_laid, ("ha", "wa"), split_axis=1, concat_axis=1, tiled=True)
    returned = returned.reshape(group_count, high_parts, wide_parts, row_steps, col_steps, channels)
    shaped = returned.reshape(
        row_groups, col_groups, high_parts, wide_parts, row_steps, col_steps, channels
    )
    shaped = shaped.transpose(4, 2, 0, 5, 3, 1, 6)
    grad_input = shaped.reshape(rows_local, cols_local, channels)
    grad_table = lax.psum(jnp.sum(table_parts, axis=0), ("ha", "wa"))
    return (grad_input, grad_table)


def solution(mesh):
    in_specs = (P("ha", "wa", None), P("ha", "wa", None), P(), P(), P(), P())
    out_specs = (P("ha", "wa", None), P())
    return jax.shard_map(body, mesh=mesh, in_specs=in_specs, out_specs=out_specs, check_vma=False)
```

profile of v0, /device:TPU:1, one launch (start us, length us, event | category | flops | bytes accessed | tf_op | source)
XLA Modules:
  0.0 330.3 jit_solution(11427729656623690947)
XLA Ops:
  0.6 1.3 reshape.82
  1.9 1.6 copy.72
  3.5 11.5 %all-to-all-start = ((bf16[2,128,2,512]{3,2,0,1:T(2,128)(2,1)}), bf16[2,128,2,512]{3,2,0,1:T(2,128)(2,1)S(1)}, u32[]{:S(2)}, u32[]{:S(2)}) async-start(bf16[2,128,2,512]{3,2,0,1:T(2,128)(2,1)} %bitcast.1), calls=%async_computation | async-start | bytes 1048576 | tf_op jit(solution)/shard_map/all_to_all | solution.py:140
  15.7 1.2 reshape.84
  17.0 1.6 copy.76
  18.6 1.0 fusion.54
  19.6 9.5 %all-to-all-done = bf16[2,128,2,512]{3,2,0,1:T(2,128)(2,1)S(1)} async-done(((bf16[2,128,2,512]{3,2,0,1:T(2,128)(2,1)}), bf16[2,128,2,512]{3,2,0,1:T(2,128)(2,1)S(1)}, u32[]{:S(2)}, u32[]{:S(2)}) %all-to-all-start) | async-done | bytes 524320 | tf_op jit(solution)/shard_map/all_to_all | solution.py:140
  29.1 4.7 %all-to-all-start.1 = ((bf16[2,128,2,512]{3,2,0,1:T(2,128)(2,1)}), bf16[2,128,2,512]{3,2,0,1:T(2,128)(2,1)}, u32[]{:S(2)}, u32[]{:S(2)}) async-start(bf16[2,128,2,512]{3,2,0,1:T(2,128)(2,1)} %bitcast.12), calls=%async_computation.1 | async-start | bytes 1048576 | tf_op jit(solution)/shard_map/all_to_all | solution.py:149
  33.8 17.4 %convolution_bitcast_fusion = f32[16,16,16,16,16]{4,3,2,1,0:T(8,128)} fusion(f32[16,16,16,31]{3,1,0,2:T(8,128)S(1)} %fusion.54, s32[16,16]{1,0:T(8,128)S(1)} %copy.74), kind=kOutput, calls=%fused_computation.64 | convolution fusion | flops 390078208 | bytes 4703232 | tf_op jit(solution)/shard_map/uve,habe->haubv/dot_general | solution.py:26
  51.2 23.5 %reshape.83 = f32[16,256,256]{2,1,0:T(8,128)} reshape(f32[16,16,16,16,16]{4,3,2,1,0:T(8,128)} %convolution_bitcast_fusion) | data formatting | bytes 8388608 | tf_op jit(solution)/shard_map/reshape | solution.py:29
  74.7 5.4 %copy.79 = f32[16,256,256]{1,2,0:T(8,128)} copy(f32[16,256,256]{2,1,0:T(8,128)} %reshape.83) | data formatting | bytes 8388608
  80.7 1.6 copy.77
  82.3 0.9 copy.80
  83.1 162.9 %while.14 = (s32[]{:T(128)}, bf16[2,256,512]{2,1,0:T(8,128)(2,1)}, f32[2,16,31,31]{2,3,1,0:T(8,128)}, bf16[2,256,512]{2,1,0:T(8,128)(2,1)S(1)}, f32[512]{0:T(512...) while((s32[]{:T(128)}, bf16[2,256,512]{2,1,0:T(8,128)(2,1)}, ...), condition=%wide.region_8.9_spmd.clone.clone, body=%wide.region_0.8_spmd.clone.clone.sunk | while | flops 1734164224 | bytes 137940368 | solution.py:136
  83.7 1.3 convolution_convert_fusion.4
  85.0 0.9 copy.105
  87.2 1.1 copy.106
  88.3 0.8 fusion.129
  89.2 1.1 copy.107
  90.3 1.1 copy.108
  91.3 2.9 convolution_add_fusion.2
  94.3 3.1 fusion.130
  97.5 5.2 %fusion.131 = bf16[16,32,256]{2,1,0:T(8,128)(2,1)} fusion(bf16[256,16,32]{0,2,1:T(8,128)(2,1)S(1)} %bitcast.193, f32[16,256]{1,0:T(8,128)S(1)} %get-tuple-element.273, f32[16,256,256]{1,2,0:T(8,128)} %copy-done.4), kind=kOutput, calls=%fused_computation.13.clone.1 | convolution fusion | flops 70390016 | bytes 4734976 | tf_op jit(solution)/shard_map/while/body/eval_jaxpr/hts,thd->shd/dot_general | solution.py:60
  102.7 3.2 multiply_reduce_fusion.2
  109.6 0.9 fusion.134
  110.5 19.4 %reshape.111 = f32[16,16,16,16,16]{2,1,4,3,0:T(8,128)} reshape(f32[16,256,256]{1,2,0:T(8,128)} %copy-done.2) | data formatting | bytes 8388608 | tf_op jit(solution)/shard_map/while/body/eval_jaxpr/reshape | solution.py:93
  129.9 30.4 %fusion.135 = f32[16,16,16,31,1]{3,1,4,2,0:T(8,128)S(1)} fusion(f32[16,16,16,16,16]{2,1,4,3,0:T(8,128)} %reshape.111, s32[16,16]{0,1:T(8,128)S(1)} %get-tuple-element.314), kind=kOutput, calls=%fused_computation.53.clone.1 | convolution fusion | flops 390086144 | bytes 4703232 | tf_op jit(solution)/shard_map/while/body/eval_jaxpr/haubv,uve->habe/dot_general | solution.py:91
  160.4 3.5 %fusion.136 = f32[2,16,31,31]{2,3,1,0:T(8,128)S(1)} fusion(f32[2,16,31,31]{2,3,1,0:T(8,128)S(1)} %copy-done.13, s32[]{:T(128)S(6)} %copy.114, f32[16,16,16,31,1]{3,1,4,2,0:T(8,128)S(1)} %fusion.135, s32[16,16]{0,1:T(8,128)S(1)} %get-tuple-element.314), kind=kOutput, calls=%fused_computation.18.clone.1 | convolution fusion | flops 47250944 | bytes 2367492 | tf_op jit(solution)/shard_map/while/body/eval_jaxpr/habe,abd->hde/dot_general | solution.py:97
  165.0 1.3 convolution_convert_fusion.4
  166.3 0.9 copy.105
  168.6 1.1 copy.106
  169.7 0.8 fusion.129
  170.5 1.1 copy.107
  171.6 1.1 copy.108
  172.7 2.9 convolution_add_fusion.2
  175.6 3.1 fusion.130
  178.8 5.2 %fusion.131 = bf16[16,32,256]{2,1,0:T(8,128)(2,1)} fusion(bf16[256,16,32]{0,2,1:T(8,128)(2,1)S(1)} %bitcast.193, f32[16,256]{1,0:T(8,128)S(1)} %get-tuple-element.273, f32[16,256,256]{1,2,0:T(8,128)} %copy-done.4), kind=kOutput, calls=%fused_computation.13.clone.1 | convolution fusion | flops 70390016 | bytes 4734976 | tf_op jit(solution)/shard_map/while/body/eval_jaxpr/hts,thd->shd/dot_general | solution.py:60
  184.0 3.2 multiply_reduce_fusion.2
  190.9 0.9 fusion.134
  191.9 19.4 %reshape.111 = f32[16,16,16,16,16]{2,1,4,3,0:T(8,128)} reshape(f32[16,256,256]{1,2,0:T(8,128)} %copy-done.2) | data formatting | bytes 8388608 | tf_op jit(solution)/shard_map/while/body/eval_jaxpr/reshape | solution.py:93
  211.3 30.4 %fusion.135 = f32[16,16,16,31,1]{3,1,4,2,0:T(8,128)S(1)} fusion(f32[16,16,16,16,16]{2,1,4,3,0:T(8,128)} %reshape.111, s32[16,16]{0,1:T(8,128)S(1)} %get-tuple-element.314), kind=kOutput, calls=%fused_computation.53.clone.1 | convolution fusion | flops 390086144 | bytes 4703232 | tf_op jit(solution)/shard_map/while/body/eval_jaxpr/haubv,uve->habe/dot_general | solution.py:91
  241.7 3.5 %fusion.136 = f32[2,16,31,31]{2,3,1,0:T(8,128)S(1)} fusion(f32[2,16,31,31]{2,3,1,0:T(8,128)S(1)} %copy-done.13, s32[]{:T(128)S(6)} %copy.114, f32[16,16,16,31,1]{3,1,4,2,0:T(8,128)S(1)} %fusion.135, s32[16,16]{0,1:T(8,128)S(1)} %get-tuple-element.314), kind=kOutput, calls=%fused_computation.18.clone.1 | convolution fusion | flops 47250944 | bytes 2367492 | tf_op jit(solution)/shard_map/while/body/eval_jaxpr/habe,abd->hde/dot_general | solution.py:97
  246.0 2.4 copy.81
  248.4 9.9 %all-to-all-start.2 = ((bf16[2,128,2,512]{3,0,2,1:T(2,128)(2,1)}), bf16[2,128,2,512]{3,0,2,1:T(2,128)(2,1)S(1)}, u32[]{:S(2)}, u32[]{:S(2)}) async-start(bf16[2,128,2,512]{3,0,2,1:T(2,128)(2,1)} %bitcast.14), calls=%async_computation.2 | async-start | bytes 1048576 | tf_op jit(solution)/shard_map/all_to_all | solution.py:167
  258.3 1.1 reduce_sum.63
  259.4 68.6 %psum.7 = f32[16,31,31]{1,2,0:T(8,128)S(1)} all-reduce(f32[16,31,31]{1,2,0:T(8,128)S(1)} %reduce_sum.63), channel_id=1, replica_groups=mesh['ha'=16,'wa'=8] {'ha','wa'}, use_global_device_ids=true, to_apply=%region_10.11 | all-reduce | flops 15376 | bytes 123008 | tf_op jit(solution)/shard_map/psum | solution.py:174
  328.0 0.9 copy.85
  329.2 1.1 copy.84
  (82 shorter events, 14.2 us)
Async XLA Ops:
  0.6 18.0 %copy-start = (f32[16,31,31]{2,0,1:T(8,128)S(1)}, f32[16,31,31]{2,0,1:T(8,128)}, u32[]{:S(2)}) copy-start(f32[16,31,31]{2,0,1:T(8,128)} %param.13) | copy-start | bytes 184516
  3.5 25.5 %all-to-all-start = ((bf16[2,128,2,512]{3,2,0,1:T(2,128)(2,1)}), bf16[2,128,2,512]{3,2,0,1:T(2,128)(2,1)S(1)}, u32[]{:S(2)}, u32[]{:S(2)}) async-start(bf16[2,128,2,512]{3,2,0,1:T(2,128)(2,1)} %bitcast.1), calls=%async_computation | async-start | bytes 1048576 | tf_op jit(solution)/shard_map/all_to_all | solution.py:140
  15.0 0.6 copy-start.11
  29.1 22.1 %copy-start.9 = (bf16[2,128,2,512]{3,2,0,1:T(2,128)(2,1)}, bf16[2,128,2,512]{3,2,0,1:T(2,128)(2,1)S(1)}, u32[]{:S(2)}) copy-start(bf16[2,128,2,512]{3,2,0,1:T(2,128)(2,1)S(1)} %all-to-all-done) | copy-start | bytes 1572868
  29.1 51.6 %all-to-all-start.1 = ((bf16[2,128,2,512]{3,2,0,1:T(2,128)(2,1)}), bf16[2,128,2,512]{3,2,0,1:T(2,128)(2,1)}, u32[]{:S(2)}, u32[]{:S(2)}) async-start(bf16[2,128,2,512]{3,2,0,1:T(2,128)(2,1)} %bitcast.12), calls=%async_computation.1 | async-start | bytes 1048576 | tf_op jit(solution)/shard_map/all_to_all | solution.py:149
  74.7 5.4 %copy-start.10 = (bf16[2,128,2,512]{3,2,0,1:T(2,128)(2,1)S(1)}, bf16[2,128,2,512]{3,2,0,1:T(2,128)(2,1)}, u32[]{:S(2)}) copy-start(bf16[2,128,2,512]{3,2,0,1:T(2,128)(2,1)} %copy-done.9) | copy-start | bytes 1572868
  80.1 3.0 copy-start.5
  80.1 3.0 copy-start.6
  80.2 3.0 copy-start.12
  80.2 3.0 copy-start.15
  94.3 3.2 copy-start.4
  94.3 3.2 copy-start.8
  102.7 3.4 %copy-start.3 = (f32[16,256,256]{1,2,0:T(8,128)S(1)}, f32[16,256,256]{1,2,0:T(8,128)}, u32[]{:S(2)}) copy-start(f32[16,256,256]{1,2,0:T(8,128)} %get-tuple-element.274) | copy-start | bytes 12582916 | tf_op jit(solution)/shard_map/while
  106.9 2.0 copy-start.2
  106.9 2.0 copy-start.16
  129.9 30.4 %copy-start.13 = (f32[2,16,31,31]{2,3,1,0:T(8,128)S(1)}, f32[2,16,31,31]{2,3,1,0:T(8,128)}, u32[]{:S(2)}) copy-start(f32[2,16,31,31]{2,3,1,0:T(8,128)} %get-tuple-element.296) | copy-start | bytes 369028 | tf_op jit(solution)/shard_map/while
  129.9 34.7 %copy-start.7 = (bf16[512,512]{1,0:T(8,128)(2,1)S(1)}, bf16[512,512]{1,0:T(8,128)(2,1)}, u32[]{:S(2)}) copy-start(bf16[512,512]{1,0:T(8,128)(2,1)} %get-tuple-element.327) | copy-start | bytes 1572868 | tf_op jit(solution)/shard_map/while
  163.9 0.8 copy-start.14
  175.6 3.2 copy-start.4
  175.6 3.2 copy-start.8
  184.0 3.4 %copy-start.3 = (f32[16,256,256]{1,2,0:T(8,128)S(1)}, f32[16,256,256]{1,2,0:T(8,128)}, u32[]{:S(2)}) copy-start(f32[16,256,256]{1,2,0:T(8,128)} %get-tuple-element.274) | copy-start | bytes 12582916 | tf_op jit(solution)/shard_map/while
  188.2 2.0 copy-start.2
  188.2 2.0 copy-start.16
  211.3 30.4 %copy-start.13 = (f32[2,16,31,31]{2,3,1,0:T(8,128)S(1)}, f32[2,16,31,31]{2,3,1,0:T(8,128)}, u32[]{:S(2)}) copy-start(f32[2,16,31,31]{2,3,1,0:T(8,128)} %get-tuple-element.296) | copy-start | bytes 369028 | tf_op jit(solution)/shard_map/while
  211.3 34.7 %copy-start.7 = (bf16[512,512]{1,0:T(8,128)(2,1)S(1)}, bf16[512,512]{1,0:T(8,128)(2,1)}, u32[]{:S(2)}) copy-start(bf16[512,512]{1,0:T(8,128)(2,1)} %get-tuple-element.327) | copy-start | bytes 1572868 | tf_op jit(solution)/shard_map/while
  245.2 0.8 copy-start.14
  246.0 84.3 %copy-start.1 = (f32[16,31,31]{2,0,1:T(8,128)S(1)}, f32[16,31,31]{2,0,1:T(8,128)}, u32[]{:S(2)}) copy-start(f32[16,31,31]{2,0,1:T(8,128)} %param.13) | copy-start | bytes 184516
  248.4 80.5 %all-to-all-start.2 = ((bf16[2,128,2,512]{3,0,2,1:T(2,128)(2,1)}), bf16[2,128,2,512]{3,0,2,1:T(2,128)(2,1)S(1)}, u32[]{:S(2)}, u32[]{:S(2)}) async-start(bf16[2,128,2,512]{3,0,2,1:T(2,128)(2,1)} %bitcast.14), calls=%async_computation.2 | async-start | bytes 1048576 | tf_op jit(solution)/shard_map/all_to_all | solution.py:167
where the time goes:
time: 332 us; the launch traced here: 330 us
  matrix products  117 us (35%)
  local copies, waits for them, and re-layouts  95.5 us (29%)
  blocking collectives  68.6 us (21%)
  starting transfers between devices  26.1 us (8%)
  other arithmetic  12.9 us (4%)
  waiting for transfers between devices  9.46 us (3%)
    psum x1, blocking collectives, body(): grad_table = lax.psum(jnp.sum(table_parts, axis=0), ('ha', 'wa'))  68.6 us
    dot_general x2, matrix products, group_grad(): jnp.einsum('haubv,uve->habe', grad_scores.reshape(HEADS, WIN, WIN, WIN, W...  60.8 us
    reshape x2, local copies, waits for them, and re-layouts, group_grad(): grad_scores.reshape(HEADS, WIN, WIN, WIN, WIN)  38.8 us
    reshape x1, local copies, waits for them, and re-layouts, full_bias(): return spread.reshape(HEADS, WIN * WIN, WIN * WIN)  23.5 us
    dot_general x1, matrix products, full_bias(): jnp.einsum('uve,habe->haubv', offset_table, partial_rows, precision=lax.P...  17.4 us
    all_to_all x1, starting transfers between devices, body(): lax.all_to_all(laid_tokens.reshape(flat_shape), ('ha', 'wa'), split_axis=...  11.5 us
    dot_general x2, matrix products, group_grad(): jnp.einsum('hts,thd->shd', probs_half, grad_out, preferred_element_type=j...  10.3 us
    all_to_all x1, starting transfers between devices, body(): lax.all_to_all(grads_laid, ('ha', 'wa'), split_axis=1, concat_axis=1, til...  9.89 us
  transfers between devices with their start and end apart: 3, of which 1 were waited for; matrix products, arithmetic and copies ran while one was open for 16% of the time, Pallas kernels for 0%

commit v1 on v0

--- a/solution.py
+++ b/solution.py
@@ -171,7 +171,7 @@
     )
     shaped = shaped.transpose(4, 2, 0, 5, 3, 1, 6)
     grad_input = shaped.reshape(rows_local, cols_local, channels)
-    grad_table = lax.psum(jnp.sum(table_parts, axis=0), ("ha", "wa"))
+    grad_table = jnp.sum(lax.all_gather(jnp.sum(table_parts, axis=0), ("ha", "wa")), axis=0)
     return (grad_input, grad_table)
 
 

time: 332 us -> 624 us (1.88)
  waiting for transfers between devices: 9.46 us -> 327 us
  blocking collectives: 68.6 us -> 26.7 us
  between operations: 0.77 us -> 14.2 us
  other arithmetic: 12.9 us -> 25.5 us
  starting transfers between devices: 26.1 us -> 16.2 us
    all_gather x0 -> x1, waiting for transfers between devices: none -> 318 us  [body(): lax.all_gather(jnp.sum(table_parts, axis=0), ('ha', 'wa'))]
    psum x1 -> x0, blocking collectives: 68.6 us -> none  [body(): grad_table = lax.psum(jnp.sum(table_parts, axis=0), ('ha', 'wa'))]
    all_to_all x0 -> x1, blocking collectives: none -> 26.7 us  [body(): lax.all_to_all(grads_laid, ('ha', 'wa'), split_axis=1, concat_axis=1, til...]
    reduce_sum x1 -> x2, other arithmetic: 1.13 us -> 13.8 us  [the longest x1 12.7 us: body(): jnp.sum(lax.all_gather(jnp.sum(table_parts, axis=0), ('ha', 'wa')), axis=0)]
    all_to_all x1 -> x0, starting transfers between devices: 9.89 us -> none  [body(): lax.all_to_all(grads_laid, ('ha', 'wa'), split_axis=1, concat_axis=1, til...]
  transfers between devices with their start and end apart: 3 -> 3, of which waited for: 1 -> 2; matrix products, arithmetic and copies ran while one was open for 16% -> 9% of each run, Pallas kernels for 0% -> 0%
where the time goes in v1:
time: 624 us; the launch traced here: 621 us
  waiting for transfers between devices  327 us (52%)
  matrix products  117 us (19%)
  local copies, waits for them, and re-layouts  94.7 us (15%)
  blocking collectives  26.7 us (4%)
  other arithmetic  25.5 us (4%)
  starting transfers between devices  16.2 us (3%)
  between operations  14.2 us (2%)
    all_gather x1, waiting for transfers between devices, body(): lax.all_gather(jnp.sum(table_parts, axis=0), ('ha', 'wa'))  318 us
    dot_general x2, matrix products, group_grad(): jnp.einsum('haubv,uve->habe', grad_scores.reshape(HEADS, WIN, WIN, WIN, W...  60.8 us
    reshape x2, local copies, waits for them, and re-layouts, group_grad(): grad_scores.reshape(HEADS, WIN, WIN, WIN, WIN)  38.8 us
    all_to_all x1, blocking collectives, body(): lax.all_to_all(grads_laid, ('ha', 'wa'), split_axis=1, concat_axis=1, til...  26.7 us
    reshape x1, local copies, waits for them, and re-layouts, full_bias(): return spread.reshape(HEADS, WIN * WIN, WIN * WIN)  23.5 us
    dot_general x1, matrix products, full_bias(): jnp.einsum('uve,habe->haubv', offset_table, partial_rows, precision=lax.P...  17.4 us
    reduce_sum x1, other arithmetic, body(): jnp.sum(lax.all_gather(jnp.sum(table_parts, axis=0), ('ha', 'wa')), axis=0)  12.7 us
  transfers between devices with their start and end apart: 3, of which 2 were waited for; matrix products, arithmetic and copies ran while one was open for 9% of the time, Pallas kernels for 0%

profile of v1, /device:TPU:1, one launch (start us, length us, event | category | flops | bytes accessed | tf_op | source)
XLA Modules:
  0.0 621.3 jit_solution(7422559573053347119)
XLA Ops:
  7.2 1.3 reshape.82
  8.5 1.6 copy.72
  10.1 11.5 %all-to-all-start = ((bf16[2,128,2,512]{3,2,0,1:T(2,128)(2,1)}), bf16[2,128,2,512]{3,2,0,1:T(2,128)(2,1)S(1)}, u32[]{:S(2)}, u32[]{:S(2)}) async-start(bf16[2,128,2,512]{3,2,0,1:T(2,128)(2,1)} %bitcast.1), calls=%async_computation | async-start | bytes 1048576 | tf_op jit(solution)/shard_map/all_to_all | solution.py:140
  22.2 1.2 reshape.84
  23.5 1.6 copy.76
  25.1 1.0 fusion.54
  26.2 9.4 %all-to-all-done = bf16[2,128,2,512]{3,2,0,1:T(2,128)(2,1)S(1)} async-done(((bf16[2,128,2,512]{3,2,0,1:T(2,128)(2,1)}), bf16[2,128,2,512]{3,2,0,1:T(2,128)(2,1)S(1)}, u32[]{:S(2)}, u32[]{:S(2)}) %all-to-all-start) | async-done | bytes 524320 | tf_op jit(solution)/shard_map/all_to_all | solution.py:140
  35.6 4.7 all-to-all-start.1
  40.4 17.4 %convolution_bitcast_fusion = f32[16,16,16,16,16]{4,3,2,1,0:T(8,128)} fusion(f32[16,16,16,31]{3,1,0,2:T(8,128)S(1)} %fusion.54, s32[16,16]{1,0:T(8,128)S(1)} %copy.74), kind=kOutput, calls=%fused_computation.64 | convolution fusion | flops 390078208 | bytes 4703232 | tf_op jit(solution)/shard_map/uve,habe->haubv/dot_general | solution.py:26
  57.8 23.5 %reshape.83 = f32[16,256,256]{2,1,0:T(8,128)} reshape(f32[16,16,16,16,16]{4,3,2,1,0:T(8,128)} %convolution_bitcast_fusion) | data formatting | bytes 8388608 | tf_op jit(solution)/shard_map/reshape | solution.py:29
  81.3 5.4 copy.79
  87.2 1.6 copy.77
  88.8 0.9 copy.80
  89.7 162.8 %while.14 = (s32[]{:T(128)}, bf16[2,256,512]{2,1,0:T(8,128)(2,1)}, f32[2,16,31,31]{2,3,1,0:T(8,128)}, bf16[2,256,512]{2,1,0:T(8,128)(2,1)S(1)}, f32[512]{0:T(512...) while((s32[]{:T(128)}, bf16[2,256,512]{2,1,0:T(8,128)(2,1)}, ...), condition=%wide.region_8.9_spmd.clone.clone, body=%wide.region_0.8_spmd.clone.clone.sunk | while | flops 1734164224 | bytes 137940368 | solution.py:136
  90.3 1.3 convolution_convert_fusion.4
  91.6 0.9 copy.105
  93.8 1.1 copy.106
  94.9 0.8 fusion.129
  95.7 1.1 copy.107
  96.8 1.1 copy.108
  97.9 2.9 convolution_add_fusion.2
  100.9 3.1 fusion.130
  104.1 5.2 fusion.131
  109.2 3.2 multiply_reduce_fusion.2
  116.2 0.9 fusion.134
  117.1 19.4 %reshape.112 = f32[16,16,16,16,16]{2,1,4,3,0:T(8,128)} reshape(f32[16,256,256]{1,2,0:T(8,128)} %copy-done.2) | data formatting | bytes 8388608 | tf_op jit(solution)/shard_map/while/body/eval_jaxpr/reshape | solution.py:93
  136.5 30.4 %fusion.135 = f32[16,16,16,31,1]{3,1,4,2,0:T(8,128)S(1)} fusion(f32[16,16,16,16,16]{2,1,4,3,0:T(8,128)} %reshape.112, s32[16,16]{0,1:T(8,128)S(1)} %get-tuple-element.314), kind=kOutput, calls=%fused_computation.53.clone.1 | convolution fusion | flops 390086144 | bytes 4703232 | tf_op jit(solution)/shard_map/while/body/eval_jaxpr/haubv,uve->habe/dot_general | solution.py:91
  166.9 3.5 fusion.136
  171.6 1.3 convolution_convert_fusion.4
  172.9 0.9 copy.105
  175.1 1.1 copy.106
  177.0 1.1 copy.107
  178.1 1.1 copy.108
  179.2 2.9 convolution_add_fusion.2
  182.2 3.1 fusion.130
  185.4 5.2 fusion.131
  190.6 3.2 multiply_reduce_fusion.2
  197.5 0.9 fusion.134
  198.4 19.4 %reshape.112 = f32[16,16,16,16,16]{2,1,4,3,0:T(8,128)} reshape(f32[16,256,256]{1,2,0:T(8,128)} %copy-done.2) | data formatting | bytes 8388608 | tf_op jit(solution)/shard_map/while/body/eval_jaxpr/reshape | solution.py:93
  217.8 30.4 %fusion.135 = f32[16,16,16,31,1]{3,1,4,2,0:T(8,128)S(1)} fusion(f32[16,16,16,16,16]{2,1,4,3,0:T(8,128)} %reshape.112, s32[16,16]{0,1:T(8,128)S(1)} %get-tuple-element.314), kind=kOutput, calls=%fused_computation.53.clone.1 | convolution fusion | flops 390086144 | bytes 4703232 | tf_op jit(solution)/shard_map/while/body/eval_jaxpr/haubv,uve->habe/dot_general | solution.py:91
  248.3 3.5 fusion.136
  252.5 1.1 reduce_sum.72
  253.7 0.9 copy.84
  254.6 1.6 copy.81
  256.2 26.7 %all_to_all.15 = bf16[2,128,2,512]{3,0,2,1:T(2,128)(2,1)S(1)} all-to-all(bf16[2,128,2,512]{3,0,2,1:T(2,128)(2,1)S(1)} %bitcast.200), channel_id=1, replica_groups=mesh['ha'=16,'wa'=8] {'ha','wa'}, dimensions={1} | all-to-all | bytes 1048576 | tf_op jit(solution)/shard_map/all_to_all | solution.py:167
  283.2 1.1 copy.85
  284.3 317.5 %all-gather.3.cloned.1.call-done = f32[2048,31,31]{2,0,1:T(8,128)} async-done(((f32[16,31,31]{2,0,1:T(8,128)}), f32[2048,31,31]{2,0,1:T(8,128)}) %all-gather.3.cloned.1.call-update) | async-done | bytes 7872528 | tf_op jit(solution)/shard_map/all_gather | solution.py:174
  601.8 12.7 %reduce_sum.73 = f32[16,31,31]{2,0,1:T(8,128)} reduce(f32[128,16,31,31]{3,1,0,2:T(8,128)} %bitcast.192, f32[]{:T(128)} %constant.34.clone.1), dimensions={0}, to_apply=%region_10.11 | reduce | flops 1952752 | bytes 7934020 | tf_op jit(solution)/shard_map/reduce_sum | solution.py:174
  (84 shorter events, 15.1 us)
Async XLA Ops:
  7.2 18.0 %copy-start = (f32[16,31,31]{2,0,1:T(8,128)S(1)}, f32[16,31,31]{2,0,1:T(8,128)}, u32[]{:S(2)}) copy-start(f32[16,31,31]{2,0,1:T(8,128)} %param.13) | copy-start | bytes 184516
  10.1 25.5 %all-to-all-start = ((bf16[2,128,2,512]{3,2,0,1:T(2,128)(2,1)}), bf16[2,128,2,512]{3,2,0,1:T(2,128)(2,1)S(1)}, u32[]{:S(2)}, u32[]{:S(2)}) async-start(bf16[2,128,2,512]{3,2,0,1:T(2,128)(2,1)} %bitcast.1), calls=%async_computation | async-start | bytes 1048576 | tf_op jit(solution)/shard_map/all_to_all | solution.py:140
  21.6 0.6 copy-start.11
  35.6 22.2 %copy-start.9 = (bf16[2,128,2,512]{3,2,0,1:T(2,128)(2,1)}, bf16[2,128,2,512]{3,2,0,1:T(2,128)(2,1)S(1)}, u32[]{:S(2)}) copy-start(bf16[2,128,2,512]{3,2,0,1:T(2,128)(2,1)S(1)} %all-to-all-done) | copy-start | bytes 1572868
  35.6 51.6 %all-to-all-start.1 = ((bf16[2,128,2,512]{3,2,0,1:T(2,128)(2,1)}), bf16[2,128,2,512]{3,2,0,1:T(2,128)(2,1)}, u32[]{:S(2)}, u32[]{:S(2)}) async-start(bf16[2,128,2,512]{3,2,0,1:T(2,128)(2,1)} %bitcast.12), calls=%async_computation.1 | async-start | bytes 1048576 | tf_op jit(solution)/shard_map/all_to_all | solution.py:149
  40.3 561.5 %all-gather.3.cloned.1.call-start = ((), (), s32[]{:S(2)}) async-start(), calls=%async_computation.3 | async-start | bytes 32759808 | tf_op jit(solution)/shard_map/all_gather | solution.py:174
  81.3 5.4 copy-start.10
  86.7 3.0 copy-start.5
  86.7 3.0 copy-start.6
  86.7 3.0 copy-start.12
  86.7 3.0 copy-start.15
  100.9 3.2 copy-start.4
  100.9 3.2 copy-start.8
  109.2 3.4 copy-start.3
  113.5 2.0 copy-start.2
  113.5 1.9 copy-start.16
  136.5 30.4 %copy-start.13 = (f32[2,16,31,31]{2,3,1,0:T(8,128)S(1)}, f32[2,16,31,31]{2,3,1,0:T(8,128)}, u32[]{:S(2)}) copy-start(f32[2,16,31,31]{2,3,1,0:T(8,128)} %get-tuple-element.296) | copy-start | bytes 369028 | tf_op jit(solution)/shard_map/while
  136.5 34.7 %copy-start.7 = (bf16[512,512]{1,0:T(8,128)(2,1)S(1)}, bf16[512,512]{1,0:T(8,128)(2,1)}, u32[]{:S(2)}) copy-start(bf16[512,512]{1,0:T(8,128)(2,1)} %get-tuple-element.329) | copy-start | bytes 1572868 | tf_op jit(solution)/shard_map/while
  170.4 0.8 copy-start.14
  182.2 3.2 copy-start.4
  182.2 3.2 copy-start.8
  190.6 3.4 copy-start.3
  194.8 2.0 copy-start.2
  194.8 1.9 copy-start.16
  217.8 30.4 %copy-start.13 = (f32[2,16,31,31]{2,3,1,0:T(8,128)S(1)}, f32[2,16,31,31]{2,3,1,0:T(8,128)}, u32[]{:S(2)}) copy-start(f32[2,16,31,31]{2,3,1,0:T(8,128)} %get-tuple-element.296) | copy-start | bytes 369028 | tf_op jit(solution)/shard_map/while
  217.8 34.7 %copy-start.7 = (bf16[512,512]{1,0:T(8,128)(2,1)S(1)}, bf16[512,512]{1,0:T(8,128)(2,1)}, u32[]{:S(2)}) copy-start(bf16[512,512]{1,0:T(8,128)(2,1)} %get-tuple-element.329) | copy-start | bytes 1572868 | tf_op jit(solution)/shard_map/while
  251.8 0.8 copy-start.14
  601.8 12.7 %copy-start.1 = (f32[16,31,31]{2,0,1:T(8,128)S(1)}, f32[16,31,31]{2,0,1:T(8,128)}, u32[]{:S(2)}) copy-start(f32[16,31,31]{2,0,1:T(8,128)} %param.13) | copy-start | bytes 184516
Sparse Core Ops, SparseCore 0:
  254.7 347.0 all-gather.2
